TPU v7x, 256 devices: a whole 4x4x8 slice. The times are simulated.
256 devices in a mesh: wide: 64 (over y, z, core), narrow: 4 (over x).
Axes of the slice: x: 4, y: 4, z: 8, core: 2. Of those that a mesh axis runs over, the one named last changes fastest.
Arguments:
- upper_panel: float32 [15360, 1024], P('wide', 'narrow'), may hold values from -0.1875 to 0.1875
- coupling: float32 [512, 512], P('wide'), may hold values from -0.25 to 0.25
- diag_inverse: float32 [2, 512, 512], replicated, as said below
- block_rhs: float32 [2, 512, 2048], P(None, 'wide'), may hold values from -6 to 6
- upper_rhs: float32 [15360, 2048], P('wide', 'narrow'), may hold values from -6 to 6
Outputs:
- solved: float32 [2, 512, 2048], P(None, 'wide', 'narrow')
- updated: float32 [15360, 2048], P('wide', 'narrow')
Inputs may be any that keep to these rules, and one draw needn't show every extreme that they name: Each diag_inverse[k] is upper triangular with a positive diagonal.
All inputs are finite; a program needn't handle non-finite values.
Results may differ from a plain program's by a relative error of at most 0.000088.
Values sent between devices are 32-bit elements; how exact they have to be, the bound alone decides.
No kernel may reach another device: no remote copies, remote signals or barrier semaphores. Data moves between devices by JAX's collectives and lax.ppermute only.
A program may use at most 64 MiB of HBM per device.

v0:
```python
import jax
import jax.numpy as jnp
from jax import lax
from jax.sharding import PartitionSpec as P


def product(left, right):
    return jnp.dot(left, right, precision=lax.Precision.HIGHEST, preferred_element_type=jnp.float32)


def local(upper_panel, coupling, diag_inverse, block_rhs, upper_rhs):
    wide_index = lax.axis_index("wide")
    narrow_index = lax.axis_index("narrow")
    block_rows = block_rhs.shape[1]
    own_targets = upper_rhs.shape[1]
    panel_width = upper_panel.shape[1]
    half_rows = diag_inverse.shape[1]
    first_rhs = block_rhs[0]
    last_rhs = block_rhs[1]

    def solve_block(inverse, local_rhs):
        return product(inverse, lax.all_gather(local_rhs, "wide", axis=0, tiled=True))

    last_block = solve_block(diag_inverse[1], last_rhs)
    first_block = solve_block(diag_inverse[0], first_rhs - product(coupling, last_block))
    stacked = jnp.concatenate([first_block, last_block], axis=0)
    matching = lax.dynamic_slice_in_dim(stacked, narrow_index * panel_width, panel_width, 0)
    partial_value = product(upper_panel, matching)
    correction = lax.psum_scatter(partial_value, "narrow", scatter_dimension=1, tiled=True)
    solved_cols = lax.dynamic_slice_in_dim(stacked, narrow_index * own_targets, own_targets, 1)
    updated = upper_rhs - correction
    first_own = lax.dynamic_slice_in_dim(
        solved_cols[:half_rows], wide_index * block_rows, block_rows, 0
    )
    last_own = lax.dynamic_slice_in_dim(
        solved_cols[half_rows:], wide_index * block_rows, block_rows, 0
    )
    solved = jnp.stack([first_own, last_own])
    return (solved, updated)


def solution(mesh):
    return jax.shard_map(
        local,
        mesh=mesh,
        in_specs=(
            P("wide", "narrow"),
            P("wide", None),
            P(),
            P(None, "wide", None),
            P("wide", "narrow"),
        ),
        out_specs=(P(None, "wide", "narrow"), P("wide", "narrow")),
        check_vma=False,
    )
```

profile of v0, /device:TPU:1, one launch (start us, length us, event | category | flops | bytes accessed | tf_op | source)
XLA Modules:
  0.0 235.7 jit_solution(2569916423738369529)
XLA Ops:
  7.2 0.0 copy-start
  7.2 0.0 all-gather.6.cloned.1.call-start
  7.2 1.5 slice.20
  8.8 0.0 all-gather.6.cloned.1.call-update
  8.8 0.0 copy-start.6
  8.8 0.0 copy-start.7
  8.8 0.0 all-gather.4.cloned.1.call-start
  8.9 85.9 %all-gather.6.cloned.1.call-done = f32[1,512,2048]{2,1,0:T(8,128)} async-done(((f32[1,8,2048]{2,1,0:T(8,128)}), f32[1,512,2048]{2,1,0:T(8,128)}) %all-gather.6.cloned.1.call-update) | async-done | bytes 4194320 | tf_op jit(solution)/shard_map/all_gather | solution.py:22
  94.8 9.1 %fusion = f32[512,2048]{1,0:T(8,128)S(1)} fusion(f32[1,512,2048]{2,1,0:T(8,128)} %all-gather.6.cloned.1.call-done, f32[2,512,512]{2,1,0:T(8,128)} %param.7), kind=kOutput, calls=%fused_computation.4 | convolution fusion | flops 6442450944 | bytes 9437184 | tf_op jit(solution)/shard_map/dot_general | solution.py:8
  103.9 2.0 copy-done.1
  105.8 2.9 %fusion.2 = f32[8,2048]{1,0:T(8,128)} fusion(f32[512,2048]{1,0:T(8,128)S(1)} %fusion, f32[8,512]{1,0:T(8,128)S(1)} %copy-done.7, f32[2,8,2048]{2,1,0:T(8,128)S(1)} %copy-done.6), kind=kOutput, calls=%fused_computation.9 | convolution fusion | flops 100679680 | bytes 4341760 | tf_op jit(solution)/shard_map/dot_general | solution.py:8
  108.8 0.0 all-gather.4.cloned.1.call-update
  108.8 0.0 reduce-scatter.2.cloned.1.call-start
  108.8 76.3 %all-gather.4.cloned.1.call-done = f32[512,2048]{1,0:T(8,128)} async-done(((f32[8,2048]{1,0:T(8,128)}), f32[512,2048]{1,0:T(8,128)}) %all-gather.4.cloned.1.call-update) | async-done | bytes 4194320 | tf_op jit(solution)/shard_map/all_gather | solution.py:22
  185.1 8.8 %convolution_bitcast_fusion = f32[512,2048]{1,0:T(8,128)S(1)} fusion(f32[512,2048]{1,0:T(8,128)} %all-gather.4.cloned.1.call-done, f32[2,512,512]{2,1,0:T(8,128)S(1)} %copy-done.4), kind=kOutput, calls=%fused_computation.6 | convolution fusion | flops 6442450944 | bytes 9437184 | tf_op jit(solution)/shard_map/dot_general | solution.py:8
  194.0 2.0 copy-done.3
  196.0 3.5 %convolution_bitcast_fusion.1 = f32[240,2048]{1,0:T(8,128)} fusion(f32[240,256]{1,0:T(8,128)S(1)} %copy-done, s32[]{:T(128)S(6)} %select_n.12, f32[512,2048]{1,0:T(8,128)S(1)} %convolution_bitcast_fusion, f32[512,2048]{1,0:T(8,128)S(1)} %copy-done.2), kind=kOutput, calls=%fused_computation.7 | convolution fusion | flops 1510473728 | bytes 10600452 | tf_op jit(solution)/shard_map/dot_general | solution.py:8
  199.5 0.0 reduce-scatter.2.cloned.1.call-update
  199.5 1.7 fusion.5
  201.2 0.0 copy-start.5
  201.2 0.2 fusion.12
  201.4 0.6 pad_maximum_fusion
  202.1 25.3 %reduce-scatter.2.cloned.1.call-done = f32[240,512]{1,0:T(8,128)} async-done(((f32[240,2048]{1,0:T(8,128)}), f32[240,512]{1,0:T(8,128)}) %reduce-scatter.2.cloned.1.call-update) | async-done | bytes 491536 | tf_op jit(solution)/shard_map/reduce_scatter | solution.py:29
  227.3 1.9 sub.7
  (11 shorter events, 0.0 us)
Async XLA Ops:
  7.2 188.8 %copy-start = (f32[240,256]{1,0:T(8,128)S(1)}, f32[240,256]{1,0:T(8,128)}, u32[]{:S(2)}) copy-start(f32[240,256]{1,0:T(8,128)} %param.5) | copy-start | bytes 737284
  7.2 87.6 %all-gather.6.cloned.1.call-start = ((), (), s32[]{:S(2)}) async-start(), calls=%async_computation.3 | async-start | bytes 4259840 | tf_op jit(solution)/shard_map/all_gather | solution.py:22
  8.8 97.0 %copy-start.6 = (f32[2,8,2048]{2,1,0:T(8,128)S(1)}, f32[2,8,2048]{2,1,0:T(8,128)}, u32[]{:S(2)}) copy-start(f32[2,8,2048]{2,1,0:T(8,128)} %param.8) | copy-start | bytes 393220
  8.8 97.0 %copy-start.7 = (f32[8,512]{1,0:T(8,128)S(1)}, f32[8,512]{1,0:T(8,128)}, u32[]{:S(2)}) copy-start(f32[8,512]{1,0:T(8,128)} %param.6) | copy-start | bytes 49156
  8.8 176.3 %all-gather.4.cloned.1.call-start = ((), (), s32[]{:S(2)}) async-start(), calls=%async_computation.1 | async-start | bytes 4259840 | tf_op jit(solution)/shard_map/all_gather | solution.py:22
  103.9 2.0 copy-start.1
  105.8 79.3 %copy-start.4 = (f32[2,512,512]{2,1,0:T(8,128)S(1)}, f32[2,512,512]{2,1,0:T(8,128)}, u32[]{:S(2)}) copy-start(f32[2,512,512]{2,1,0:T(8,128)} %param.7) | copy-start | bytes 6291460
  108.8 118.6 %reduce-scatter.2.cloned.1.call-start = ((), (), s32[]{:S(2)}) async-start(), calls=%async_computation.2 | async-start | bytes 2457600 | tf_op jit(solution)/shard_map/reduce_scatter | solution.py:29
  185.1 10.8 %copy-start.2 = (f32[512,2048]{1,0:T(8,128)S(1)}, f32[512,2048]{1,0:T(8,128)}, u32[]{:S(2)}) copy-start(f32[512,2048]{1,0:T(8,128)} %copy-done.1) | copy-start | bytes 12582916
  194.0 2.0 copy-start.3
  201.2 26.1 %copy-start.5 = (f32[240,512]{1,0:T(8,128)S(1)}, f32[240,512]{1,0:T(8,128)}, u32[]{:S(2)}) copy-start(f32[240,512]{1,0:T(8,128)} %param.9) | copy-start | bytes 1474564
Sparse Core Ops, SparseCore 0:
  11.3 83.4 all-gather.5
  108.9 76.1 all-gather.3
  199.6 27.6 reduce-scatter.1
where the time goes:
time: 236 us
  waiting for transfers between devices  188 us (80%)
  matrix products  24.3 us (10%)
  between operations  13.8 us (6%)
  local copies, waits for them, and re-layouts  5.69 us (2%)
  other arithmetic  4.22 us (2%)
    all_gather x2, waiting for transfers between devices, solve_block(): lax.all_gather(local_rhs, 'wide', axis=0, tiled=True)  162 us
    reduce_scatter x1, waiting for transfers between devices, local(): lax.psum_scatter(partial_value, 'narrow', scatter_dimension=1, tiled=True)  25.3 us
    dot_general x4, matrix products, product(): jnp.dot(left, right, precision=lax.Precision.HIGHEST, preferred_element_t...  24.3 us
  transfers between devices with their start and end apart: 3, of which 3 were waited for; matrix products, arithmetic and copies ran while one was open for 1% of the time, Pallas kernels for 0%

commit v1 on v0

--- a/solution.py
+++ b/solution.py
@@ -19,7 +19,14 @@
     last_rhs = block_rhs[1]
 
     def solve_block(inverse, local_rhs):
-        return product(inverse, lax.all_gather(local_rhs, "wide", axis=0, tiled=True))
+
+        def refer_members_all_on_mesh(incoming_x):
+            parts_seen = []
+            for _ in range(lax.psum(1, "wide")):
+                parts_seen.append(incoming_x)
+            return jnp.concatenate(lax.all_to_all(jnp.stack(parts_seen, 0), "wide", 0, 0), 0)
+
+        return product(inverse, refer_members_all_on_mesh(local_rhs))
 
     last_block = solve_block(diag_inverse[1], last_rhs)
     first_block = solve_block(diag_inverse[0], first_rhs - product(coupling, last_block))

time: 236 us -> 285 us (1.21)
  blocking collectives: 0 us -> 109 us
  waiting for transfers between devices: 188 us -> 121 us
  starting transfers between devices: 0.12 us -> 6.24 us
    all_gather x2 -> x0, waiting for transfers between devices: 162 us -> none  [solve_block(): lax.all_gather(local_rhs, 'wide', axis=0, tiled=True)]
    all_to_all x0 -> x1, blocking collectives: none -> 109 us  [refer_members_all_on_mesh(): lax.all_to_all(jnp.stack(parts_seen, 0), 'wide', 0, 0)]
    all_to_all x0 -> x1, waiting for transfers between devices: none -> 95.6 us  [refer_members_all_on_mesh(): lax.all_to_all(jnp.stack(parts_seen, 0), 'wide', 0, 0)]
    all_to_all x0 -> x1, starting transfers between devices: none -> 6.02 us  [refer_members_all_on_mesh(): lax.all_to_all(jnp.stack(parts_seen, 0), 'wide', 0, 0)]
    another operation x0 -> x2, local copies, waits for them, and re-layouts: none -> 2.96 us  [refer_members_all_on_mesh(): jnp.stack(parts_seen, 0)]
  transfers between devices with their start and end apart: 3 -> 2, of which waited for: 3 -> 2; matrix products, arithmetic and copies ran while one was open for 1% -> 1% of each run, Pallas kernels for 0% -> 0%
where the time goes in v1:
time: 285 us; the launch traced here: 284 us
  waiting for transfers between devices  121 us (42%)
  blocking collectives  109 us (38%)
  matrix products  21.7 us (8%)
  between operations  14.1 us (5%)
  local copies, waits for them, and re-layouts  7.97 us (3%)
  starting transfers between devices  6.24 us (2%)
  other arithmetic  4.22 us (1%)
    all_to_all x1, blocking collectives, refer_members_all_on_mesh(): lax.all_to_all(jnp.stack(parts_seen, 0), 'wide', 0, 0)  109 us
    all_to_all x1, waiting for transfers between devices, refer_members_all_on_mesh(): lax.all_to_all(jnp.stack(parts_seen, 0), 'wide', 0, 0)  95.6 us
    reduce_scatter x1, waiting for transfers between devices, local(): lax.psum_scatter(partial_value, 'narrow', scatter_dimension=1, tiled=True)  25.1 us
    dot_general x4, matrix products, product(): jnp.dot(left, right, precision=lax.Precision.HIGHEST, preferred_element_t...  21.7 us
    all_to_all x1, starting transfers between devices, refer_members_all_on_mesh(): lax.all_to_all(jnp.stack(parts_seen, 0), 'wide', 0, 0)  6.02 us
  transfers between devices with their start and end apart: 2, of which 2 were waited for; matrix products, arithmetic and copies ran while one was open for 1% of the time, Pallas kernels for 0%

profile of v1, /device:TPU:1, one launch (start us, length us, event | category | flops | bytes accessed | tf_op | source)
XLA Modules:
  0.0 284.2 jit_solution(7767497454436882229)
XLA Ops:
  7.2 0.0 copy-start
  7.2 0.9 slice_bitcast_fusion
  8.1 0.5 stack.10
  8.6 0.0 copy-start.4
  8.6 109.2 %all_to_all.10 = f32[64,8,2048]{2,1,0:T(8,128)S(1)} all-to-all(f32[64,8,2048]{2,1,0:T(8,128)S(1)} %stack.10), channel_id=1, replica_groups=mesh['wide'=64,'narrow'=4] {'wide'}, dimensions={0} | all-to-all | bytes 8388608 | tf_op jit(solution)/shard_map/all_to_all | solution.py:27
  117.8 0.0 copy-done.4
  117.8 7.1 %fusion.2 = f32[512,2048]{1,0:T(8,128)S(1)} fusion(f32[64,8,2048]{2,1,0:T(8,128)S(1)} %all_to_all.10, f32[2,512,512]{2,1,0:T(8,128)S(1)} %copy-done.4), kind=kOutput, calls=%fused_computation.6 | convolution fusion | flops 6442450944 | bytes 9437184 | tf_op jit(solution)/shard_map/dot_general | solution.py:8
  124.9 0.0 copy-start.1
  124.9 1.9 copy-done.1
  126.9 2.3 fusion.7
  129.2 2.5 stack.11
  131.6 6.0 %all-to-all-start.1 = ((f32[64,8,2048]{2,1,0:T(8,128)}), f32[64,8,2048]{2,1,0:T(8,128)}, u32[]{:S(2)}, u32[]{:S(2)}) async-start(f32[64,8,2048]{2,1,0:T(8,128)} %stack.11), calls=%async_computation.1 | async-start | bytes 8388608 | tf_op jit(solution)/shard_map/all_to_all | solution.py:27
  137.7 0.2 reduce-scatter.2.cloned.1.call-start
  137.9 95.6 %all-to-all-done.1 = f32[64,8,2048]{2,1,0:T(8,128)} async-done(((f32[64,8,2048]{2,1,0:T(8,128)}), f32[64,8,2048]{2,1,0:T(8,128)}, u32[]{:S(2)}, u32[]{:S(2)}) %all-to-all-start.1) | async-done | bytes 4194336 | tf_op jit(solution)/shard_map/all_to_all | solution.py:27
  233.5 8.8 %fusion.4 = f32[512,2048]{1,0:T(8,128)S(1)} fusion(f32[64,8,2048]{2,1,0:T(8,128)} %all-to-all-done.1, f32[2,512,512]{2,1,0:T(8,128)S(1)} %copy-done.4), kind=kOutput, calls=%fused_computation.8 | convolution fusion | flops 6442450944 | bytes 9437184 | tf_op jit(solution)/shard_map/dot_general | solution.py:8
  242.4 2.0 copy-done.3
  244.3 3.5 %convolution_bitcast_fusion = f32[240,2048]{1,0:T(8,128)} fusion(f32[240,256]{1,0:T(8,128)S(1)} %copy-done, s32[]{:T(128)S(6)} %select_n.12, f32[512,2048]{1,0:T(8,128)S(1)} %fusion.4, f32[512,2048]{1,0:T(8,128)S(1)} %copy-done.2), kind=kOutput, calls=%fused_computation.9 | convolution fusion | flops 1510473728 | bytes 10600452 | tf_op jit(solution)/shard_map/dot_general | solution.py:8
  247.8 0.0 reduce-scatter.2.cloned.1.call-update
  247.8 1.7 fusion.10
  249.6 0.0 copy-start.5
  249.6 0.2 fusion.17
  249.8 0.6 pad_maximum_fusion
  250.4 25.1 %reduce-scatter.2.cloned.1.call-done = f32[240,512]{1,0:T(8,128)} async-done(((f32[240,2048]{1,0:T(8,128)}), f32[240,512]{1,0:T(8,128)}) %reduce-scatter.2.cloned.1.call-update) | async-done | bytes 491536 | tf_op jit(solution)/shard_map/reduce_scatter | solution.py:36
  275.5 1.9 sub.7
  (10 shorter events, 0.0 us)
Async XLA Ops:
  7.2 237.2 %copy-start = (f32[240,256]{1,0:T(8,128)S(1)}, f32[240,256]{1,0:T(8,128)}, u32[]{:S(2)}) copy-start(f32[240,256]{1,0:T(8,128)} %param.5) | copy-start | bytes 737284
  8.6 109.2 %copy-start.4 = (f32[2,512,512]{2,1,0:T(8,128)S(1)}, f32[2,512,512]{2,1,0:T(8,128)}, u32[]{:S(2)}) copy-start(f32[2,512,512]{2,1,0:T(8,128)} %param.7) | copy-start | bytes 6291460
  117.8 9.1 %copy-start.6 = (f32[2,8,2048]{2,1,0:T(8,128)S(1)}, f32[2,8,2048]{2,1,0:T(8,128)}, u32[]{:S(2)}) copy-start(f32[2,8,2048]{2,1,0:T(8,128)} %param.8) | copy-start | bytes 393220
  117.8 9.1 %copy-start.7 = (f32[8,512]{1,0:T(8,128)S(1)}, f32[8,512]{1,0:T(8,128)}, u32[]{:S(2)}) copy-start(f32[8,512]{1,0:T(8,128)} %param.6) | copy-start | bytes 49156
  124.9 2.0 copy-start.1
  131.6 101.9 %all-to-all-start.1 = ((f32[64,8,2048]{2,1,0:T(8,128)}), f32[64,8,2048]{2,1,0:T(8,128)}, u32[]{:S(2)}, u32[]{:S(2)}) async-start(f32[64,8,2048]{2,1,0:T(8,128)} %stack.11), calls=%async_computation.1 | async-start | bytes 8388608 | tf_op jit(solution)/shard_map/all_to_all | solution.py:27
  137.7 137.8 %reduce-scatter.2.cloned.1.call-start = ((), (), s32[]{:S(2)}) async-start(), calls=%async_computation.3 | async-start | bytes 2457600 | tf_op jit(solution)/shard_map/reduce_scatter | solution.py:36
  233.5 10.8 %copy-start.2 = (f32[512,2048]{1,0:T(8,128)S(1)}, f32[512,2048]{1,0:T(8,128)}, u32[]{:S(2)}) copy-start(f32[512,2048]{1,0:T(8,128)} %copy-done.1) | copy-start | bytes 12582916
  242.4 2.0 copy-start.3
  249.6 25.9 %copy-start.5 = (f32[240,512]{1,0:T(8,128)S(1)}, f32[240,512]{1,0:T(8,128)}, u32[]{:S(2)}) copy-start(f32[240,512]{1,0:T(8,128)} %param.9) | copy-start | bytes 1474564
Sparse Core Ops, SparseCore 0:
  247.9 27.5 reduce-scatter.1
